TPU v7x, 128 devices: a whole 4x4x4 slice. The times are simulated.
128 devices in a mesh: grid: 4 (over y), ens: 32 (over x, z, core).
Axes of the slice: x: 4, y: 4, z: 4, core: 2. Of those that a mesh axis runs over, the one named last changes fastest.
Arguments:
- snapshots: bfloat16 [4096, 32768], P('ens', 'grid'), may hold values from -32 to 32
- tile_mask: int32 [64, 5], P('grid'), may hold values from 0 to 1, as said below
- kernels: bfloat16 [5, 512, 512], replicated, may hold values from -2 to 2
- test_matrix: bfloat16 [4096, 256], P('ens'), may hold values from -0.09375 to 0.09375
Outputs:
- basis: float32 [32768, 256], P(('grid', 'ens'))
- coefficients: float32 [4096, 256], P('ens')
Inputs may be any that keep to these rules, and one draw needn't show every extreme that they name: `tile_mask`: the middle diagonal (index 2) is present in every tile row.
All inputs are finite; a program needn't handle non-finite values.
Results may differ from a plain program's by a relative error of at most 0.0033.
Values may be sent and summed in bfloat16 or wider, within the bound.
A program may use at most 64 MiB of HBM per device.

v0:
```python
import math

import jax
import jax.numpy as jnp
from jax import lax
from jax.sharding import PartitionSpec as P


def padded_2(block, sides, width):
    for axis, dim in sides:
        count = lax.axis_size(axis)
        forward = [(i, i + 1) for i in range(count - 1)]
        backward = [(target, source) for source, target in forward]
        low = lax.ppermute(
            lax.slice_in_dim(block, block.shape[dim] - width, None, axis=dim), axis, forward
        )
        high = lax.ppermute(lax.slice_in_dim(block, 0, width, axis=dim), axis, backward)
        block = jnp.concatenate([low, block, high], axis=dim)
    return block


def localize(anomaly, tile_mask, kernels):
    diags = kernels.shape[0]
    half = diags // 2
    tile_width = kernels.shape[1]
    scen_dev = anomaly.shape[0]
    tiles_dev = tile_mask.shape[0]
    padded = padded_2(anomaly, (("grid", 1),), half * tile_width)
    tiles = padded.reshape(scen_dev, tiles_dev + 2 * half, tile_width)
    total = jnp.zeros((scen_dev, tiles_dev, tile_width), jnp.float32)
    for diag in range(diags):
        prod = jnp.einsum(
            "sit,tu->siu",
            tiles[:, diag : diag + tiles_dev],
            kernels[diag],
            preferred_element_type=jnp.float32,
        )
        total = total + prod * tile_mask[:, diag].astype(jnp.float32)[None, :, None]
    return total.reshape(scen_dev, tiles_dev * tile_width).astype(jnp.bfloat16)


def orthonormal(span):
    local_gram = lax.dot_general(
        span, span, (((0,), (0,)), ((), ())), precision=lax.Precision.HIGHEST
    )
    gram = lax.psum(local_gram, ("grid", "ens"))
    lower = jnp.linalg.cholesky(gram)
    return jax.scipy.linalg.solve_triangular(lower, span.T, lower=True).T


def scenario_span(fields, mixing):
    return lax.psum_scatter(
        lax.dot_general(
            fields, mixing, (((0,), (0,)), ((), ())), preferred_element_type=jnp.float32
        ),
        "ens",
        scatter_dimension=0,
        tiled=True,
    )


def scenario_weights(fields, basis_half):
    partial_value = jnp.dot(
        fields,
        lax.all_gather(basis_half, "ens", axis=0, tiled=True),
        preferred_element_type=jnp.float32,
    )
    return lax.psum(partial_value, "grid")


def per_device(snapshots, tile_mask, kernels, test_matrix):
    scen_dev = snapshots.shape[0]
    groups = lax.axis_size("ens")
    total_scen = scen_dev * groups
    total_cells = snapshots.shape[1] * lax.axis_size("grid")
    rank_width = test_matrix.shape[1]
    column = jnp.sum(snapshots, axis=0, dtype=jnp.float32)
    means = lax.psum(column, "ens") / total_scen
    anomaly = (snapshots.astype(jnp.float32) - means[None, :]).astype(jnp.bfloat16)
    fields = localize(anomaly, tile_mask, kernels)
    first_basis = orthonormal(scenario_span(fields, test_matrix)).astype(jnp.bfloat16)
    weights = scenario_weights(fields, first_basis).astype(jnp.bfloat16)
    second_basis = orthonormal(scenario_span(fields, weights))
    coefficients = scenario_weights(fields, second_basis.astype(jnp.bfloat16))
    basis = second_basis * math.sqrt(total_cells)
    coefficients = coefficients * math.sqrt(rank_width / total_cells)
    return (basis, coefficients)


def solution(mesh):
    return jax.shard_map(
        per_device,
        mesh=mesh,
        in_specs=(P("ens", "grid"), P("grid", None), P(), P("ens", None)),
        out_specs=(P(("grid", "ens"), None), P("ens", None)),
        check_vma=False,
    )
```

profile of v0, /device:TPU:0, one launch (start us, length us, event | category | flops | bytes accessed | tf_op | source)
XLA Modules:
  0.0 956.5 jit_solution(13966422973999442182)
XLA Ops:
  11.1 129.5 %psum.35 = f32[8192]{0:T(1024)S(1)} all-reduce(f32[8192]{0:T(1024)S(1)} %convert_reduce_fusion), channel_id=1, replica_groups=mesh['grid'=4,'ens'=32] {'ens'}, use_global_device_ids=true, to_apply=%region_1.0 | all-reduce | flops 8192 | bytes 65536 | tf_op jit(solution)/shard_map/psum | solution.py:78
  151.5 4.4 collective-permute-done.1
  155.9 7.7 pad_maximum_fusion
  175.5 4.5 fusion.43
  180.2 89.0 %reduce-scatter.3.cloned.1.call-done = f32[256,256]{1,0:T(8,128)} async-done(((f32[8192,256]{1,0:T(8,128)}), f32[256,256]{1,0:T(8,128)}) %reduce-scatter.3.cloned.1.call-update) | async-done | bytes 262160 | tf_op jit(solution)/shard_map/reduce_scatter | solution.py:52
  271.6 145.3 %all-reduce.6.cloned.1.call-done = f32[256,256]{0,1:T(8,128)} async-done(((f32[256,256]{0,1:T(8,128)}), f32[256,256]{0,1:T(8,128)}) %all-reduce.6.cloned.1.call-update) | async-done | bytes 262160 | tf_op jit(solution)/shard_map/psum | solution.py:46
  419.0 11.7 %cholesky.130 = f32[128,128]{1,0:T(8,128)S(1)} custom-call(f32[128,128]{1,0:T(8,128)S(1)} %cholesky.194), custom_call_target="Cholesky" | custom-call | tf_op jit(solution)/shard_map/jit(cholesky)/cholesky | solution.py:47
  430.8 9.8 %custom-call.13 = f32[1,128,128]{1,2,0:T(8,128)S(1)} custom-call(f32[1,128,128]{2,1,0:T(8,128)S(1)} %get-tuple-element.53), custom_call_target="InvertDiagBlocksLowerTriangular" | custom-call | tf_op jit(solution)/shard_map/jit(cholesky)/cholesky | solution.py:47
  441.1 11.7 %cholesky.147 = f32[128,128]{1,0:T(8,128)S(1)} custom-call(f32[128,128]{1,0:T(8,128)S(1)} %convolution_subtract_fusion.3), custom_call_target="Cholesky" | custom-call | tf_op jit(solution)/shard_map/jit(cholesky)/cholesky | solution.py:47
  455.0 4.3 while.4
  459.3 19.7 %custom-call.14 = f32[2,128,128]{1,2,0:T(8,128)S(1)} custom-call(f32[2,128,128]{2,1,0:T(8,128)S(1)} %get-tuple-element.18), custom_call_target="InvertDiagBlocksLowerTriangular" | custom-call | tf_op jit(solution)/shard_map/jit(_solve_triangular)/triangular_solve | solution.py:48
  480.8 46.2 %all-gather.3.cloned.1.call-done = bf16[8192,256]{0,1:T(8,128)(2,1)} async-done(((bf16[256,256]{0,1:T(8,128)(2,1)}), bf16[8192,256]{0,1:T(8,128)(2,1)}) %all-gather.3.cloned.1.call-update) | async-done | bytes 4194320 | tf_op jit(solution)/shard_map/all_gather | solution.py:65
  530.7 18.4 %all-reduce.11 = bf16[128,256]{1,0:T(8,128)(2,1)S(1)} all-reduce(f32[128,256]{1,0:T(8,128)S(1)} %fusion.45), channel_id=1, replica_groups=mesh['grid'=4,'ens'=32] {'grid'}, use_global_device_ids=true, to_apply=%region_8.11 | all-reduce | flops 32768 | bytes 196608 | tf_op jit(solution)/shard_map/psum | solution.py:68
  549.0 4.5 fusion.48
  553.6 90.9 %reduce-scatter.5.cloned.1.call-done = f32[256,256]{1,0:T(8,128)} async-done(((f32[8192,256]{1,0:T(8,128)}), f32[256,256]{1,0:T(8,128)}) %reduce-scatter.5.cloned.1.call-update) | async-done | bytes 262160 | tf_op jit(solution)/shard_map/reduce_scatter | solution.py:52
  647.0 145.1 %all-reduce.8.cloned.1.call-done = f32[256,256]{0,1:T(8,128)} async-done(((f32[256,256]{0,1:T(8,128)}), f32[256,256]{0,1:T(8,128)}) %all-reduce.8.cloned.1.call-update) | async-done | bytes 262160 | tf_op jit(solution)/shard_map/psum | solution.py:46
  794.1 11.7 %cholesky.164 = f32[128,128]{1,0:T(8,128)S(1)} custom-call(f32[128,128]{1,0:T(8,128)S(1)} %cholesky.197), custom_call_target="Cholesky" | custom-call | tf_op jit(solution)/shard_map/jit(cholesky)/cholesky | solution.py:47
  805.9 9.8 %custom-call.15 = f32[1,128,128]{1,2,0:T(8,128)S(1)} custom-call(f32[1,128,128]{2,1,0:T(8,128)S(1)} %get-tuple-element.49), custom_call_target="InvertDiagBlocksLowerTriangular" | custom-call | tf_op jit(solution)/shard_map/jit(cholesky)/cholesky | solution.py:47
  816.2 11.7 %cholesky.181 = f32[128,128]{1,0:T(8,128)S(1)} custom-call(f32[128,128]{1,0:T(8,128)S(1)} %convolution_subtract_fusion.2), custom_call_target="Cholesky" | custom-call | tf_op jit(solution)/shard_map/jit(cholesky)/cholesky | solution.py:47
  830.6 4.3 while.5
  834.9 19.7 %custom-call.16 = f32[2,128,128]{1,2,0:T(8,128)S(1)} custom-call(f32[2,128,128]{2,1,0:T(8,128)S(1)} %get-tuple-element.19), custom_call_target="InvertDiagBlocksLowerTriangular" | custom-call | tf_op jit(solution)/shard_map/jit(_solve_triangular)/triangular_solve | solution.py:48
  856.3 46.2 %all-gather.5.cloned.1.call-done = bf16[8192,256]{0,1:T(8,128)(2,1)} async-done(((bf16[256,256]{0,1:T(8,128)(2,1)}), bf16[8192,256]{0,1:T(8,128)(2,1)}) %all-gather.5.cloned.1.call-update) | async-done | bytes 4194320 | tf_op jit(solution)/shard_map/all_gather | solution.py:65
  902.5 4.4 fusion.47
  907.7 40.1 %all-reduce.10.cloned.1.call-done = f32[128,256]{1,0:T(8,128)} async-done(((f32[128,256]{1,0:T(8,128)}), f32[128,256]{1,0:T(8,128)}) %all-reduce.10.cloned.1.call-update) | async-done | bytes 131088 | tf_op jit(solution)/shard_map/psum | solution.py:68
  (90 shorter events, 56.9 us)
Async XLA Ops:
  7.2 168.3 %copy-start = (bf16[128,256]{1,0:T(8,128)(2,1)S(1)}, bf16[128,256]{1,0:T(8,128)(2,1)}, u32[]{:S(2)}) copy-start(bf16[128,256]{1,0:T(8,128)(2,1)} %param.10) | copy-start | bytes 196612
  7.2 262.0 %reduce-scatter.3.cloned.1.call-start = ((), (), s32[]{:S(2)}) async-start(), calls=%async_computation.2 | async-start | bytes 8650752 | tf_op jit(solution)/shard_map/reduce_scatter | solution.py:52
  140.6 8.8 copy-start.4
  144.1 7.4 collective-permute-start
  147.6 8.3 collective-permute-start.1
  149.5 14.1 %copy-start.1 = (bf16[5,512,512]{2,1,0:T(8,128)(2,1)S(1)}, bf16[5,512,512]{2,1,0:T(8,128)(2,1)}, u32[]{:S(2)}) copy-start(bf16[5,512,512]{2,1,0:T(8,128)(2,1)} %param.9) | copy-start | bytes 7864324
  179.9 237.0 %all-reduce.6.cloned.1.call-start = ((), (), s32[]{:S(2)}) async-start(), calls=%async_computation.3 | async-start | bytes 524288 | tf_op jit(solution)/shard_map/psum | solution.py:46
  269.1 209.9 %copy-start.2 = (f32[256,256]{1,0:T(8,128)S(1)}, f32[256,256]{1,0:T(8,128)}, u32[]{:S(2)}) copy-start(f32[256,256]{1,0:T(8,128)} %reduce-scatter.3.cloned.1.call-done) | copy-start | bytes 786436
  271.6 255.4 %all-gather.3.cloned.1.call-start = ((), (), s32[]{:S(2)}) async-start(), calls=%async_computation.4 | async-start | bytes 4325376 | tf_op jit(solution)/shard_map/all_gather | solution.py:65
  480.8 163.7 %reduce-scatter.5.cloned.1.call-start = ((), (), s32[]{:S(2)}) async-start(), calls=%async_computation.5 | async-start | bytes 8650752 | tf_op jit(solution)/shard_map/reduce_scatter | solution.py:52
  553.5 238.5 %all-reduce.8.cloned.1.call-start = ((), (), s32[]{:S(2)}) async-start(), calls=%async_computation.6 | async-start | bytes 524288 | tf_op jit(solution)/shard_map/psum | solution.py:46
  644.5 210.0 %copy-start.3 = (f32[256,256]{1,0:T(8,128)S(1)}, f32[256,256]{1,0:T(8,128)}, u32[]{:S(2)}) copy-start(f32[256,256]{1,0:T(8,128)} %reduce-scatter.5.cloned.1.call-done) | copy-start | bytes 786436
  646.9 255.6 %all-gather.5.cloned.1.call-start = ((), (), s32[]{:S(2)}) async-start(), calls=%async_computation.7 | async-start | bytes 4325376 | tf_op jit(solution)/shard_map/all_gather | solution.py:65
  856.3 91.6 %all-reduce.10.cloned.1.call-start = ((), (), s32[]{:S(2)}) async-start(), calls=%async_computation.8 | async-start | bytes 262144 | tf_op jit(solution)/shard_map/psum | solution.py:68
Sparse Core Ops, SparseCore 0:
  180.1 89.0 reduce-scatter.2
  274.5 142.4 all-reduce.5
  480.9 46.0 all-gather.2
  553.6 90.8 reduce-scatter.4
  649.7 142.3 all-reduce.7
  856.4 46.0 all-gather.4
  907.0 40.8 all-reduce.9
where the time goes:
time: 960 us; the launch traced here: 957 us
  waiting for transfers between devices  609 us (63%)
  blocking collectives  148 us (15%)
  other arithmetic  125 us (13%)
  matrix products  33.6 us (4%)
  local copies, waits for them, and re-layouts  17.5 us (2%)
  between operations  17.4 us (2%)
    psum x2, waiting for transfers between devices, orthonormal(): gram = lax.psum(local_gram, ('grid', 'ens'))  290 us
    reduce_scatter x2, waiting for transfers between devices, scenario_span(): lax.psum_scatter(lax.dot_general(fields, mixing, (((0,), (0,)), ((), ()))...  180 us
    psum x1, blocking collectives, per_device(): means = lax.psum(column, 'ens') / total_scen  130 us
    all_gather x2, waiting for transfers between devices, scenario_weights(): lax.all_gather(basis_half, 'ens', axis=0, tiled=True)  92.3 us
    another operation x13, other arithmetic, orthonormal(): lower = jnp.linalg.cholesky(gram)  68.6 us
    psum x1, waiting for transfers between devices, scenario_weights(): return lax.psum(partial_value, 'grid')  40.1 us
    another operation x5, other arithmetic, orthonormal(): return jax.scipy.linalg.solve_triangular(lower, span.T, lower=True).T  39.4 us
  transfers between devices with their start and end apart: 9, of which 9 were waited for; matrix products, arithmetic and copies ran while one was open for 0% of the time, Pallas kernels for 0%

commit v1 on v0

v1 whole, which is shorter than its diff:
```python
import functools
import math

import jax
import jax.numpy as jnp
from jax import lax
from jax.experimental import pallas as pl
from jax.experimental.pallas import tpu as pltpu
from jax.sharding import PartitionSpec as P

MESH = pl.DeviceIdType.MESH
HIGHEST = lax.Precision.HIGHEST
VMEM = pl.BlockSpec(memory_space=pltpu.VMEM)
ANY = pl.BlockSpec(memory_space=pl.ANY)
NX, NZ, NCORE, NY = 4, 4, 2, 4
PLANE = NX * NZ * NCORE
LIMIT = 60 * 1024 * 1024


def place():
    me = lax.axis_index("ens")
    return me, me // (NZ * NCORE), (me // NCORE) % NZ, me % NCORE


def greet(peers):
    barrier = pltpu.get_barrier_semaphore()
    for peer in peers:
        pl.semaphore_signal(barrier, inc=1, device_id=peer, device_id_type=MESH)
    pl.semaphore_wait(barrier, len(peers))


def greet_plane(me, others=()):
    barrier = pltpu.get_barrier_semaphore()

    def one(k, carry):
        peer = (me + k) % PLANE
        pl.semaphore_signal(barrier, inc=1, device_id={"ens": peer}, device_id_type=MESH)
        return carry

    lax.fori_loop(1, PLANE, one, 0)
    for peer in others:
        pl.semaphore_signal(barrier, inc=1, device_id=peer, device_id_type=MESH)
    pl.semaphore_wait(barrier, PLANE - 1 + len(others))


def remote(src, dst, send, recv, peer):
    return pltpu.make_async_remote_copy(
        src_ref=src, dst_ref=dst, send_sem=send, recv_sem=recv, device_id=peer, device_id_type=MESH
    )


def each(low, high, body):
    def step(k, carry):
        body(k)
        return carry

    lax.fori_loop(low, high, step, 0)


def exchange_kernel(local_ref, means_ref, out_ref, all_means_ref, own_sem, send, recv, msend, mrecv):
    me = lax.axis_index("ens")
    width = out_ref.shape[2]
    greet_plane(me)

    def columns(owner):
        return pl.ds(pl.multiple_of(owner * width, width), width)

    def copies(k):
        peer = {"ens": (me + k) % PLANE}
        cols = columns((me + k) % PLANE)
        return (
            remote(means_ref.at[:, cols], all_means_ref.at[me], msend.at[k], mrecv.at[k], peer),
            remote(local_ref.at[:, cols], out_ref.at[me], send.at[k], recv.at[k], peer),
        )

    def start(k):
        for copy in copies(k):
            copy.start()

    each(1, PLANE, start)
    own = (
        pltpu.make_async_copy(local_ref.at[:, columns(me)], out_ref.at[me], own_sem.at[0]),
        pltpu.make_async_copy(means_ref.at[:, columns(me)], all_means_ref.at[me], own_sem.at[1]),
    )
    for copy in own:
        copy.start()
    for copy in own:
        copy.wait()

    def finish(k):
        for copy in copies(k):
            copy.wait()

    each(1, PLANE, finish)


def exchange(local, means):
    scen, cells = local.shape
    width = cells // PLANE
    return pl.pallas_call(
        exchange_kernel,
        out_shape=(
            jax.ShapeDtypeStruct((PLANE, scen, width), local.dtype),
            jax.ShapeDtypeStruct((PLANE, means.shape[0], width), means.dtype),
        ),
        in_specs=[VMEM, VMEM],
        out_specs=(VMEM, VMEM),
        scratch_shapes=[pltpu.SemaphoreType.DMA((2,))] + [pltpu.SemaphoreType.DMA((PLANE,))] * 4,
        compiler_params=pltpu.CompilerParams(collective_id=0, has_side_effects=True, vmem_limit_bytes=LIMIT),
        name="exchange",
    )(local, means)


def gather_kernel(own_ref, out_ref, own_sem, send, recv, core_send, core_recv):
    me, x, z, c = place()
    half = own_ref.shape[1] // 2
    xs = [((x + k) % NX) for k in range(1, NX)]
    zs = [((z + k) % NZ) for k in range(1, NZ)]
    xpeers = [{"ens": v * NZ * NCORE + z * NCORE + c} for v in xs]
    zpeers = [{"ens": x * NZ * NCORE + v * NCORE + c} for v in zs]
    twin = {"ens": me + 1 - 2 * c}
    greet(xpeers + zpeers + [twin])
    left, right = pl.ds(0, half), pl.ds(half, half)
    first = []
    for k in range(NX - 1):
        first.append(remote(own_ref.at[:, left], out_ref.at[x, z, c, :, left], send.at[0, k], recv.at[0, k], xpeers[k]))
        first.append(remote(own_ref.at[:, right], out_ref.at[x, z, c, :, right], send.at[1, k], recv.at[1, k], zpeers[k]))
    for copy in first:
        copy.start()
    mine = pltpu.make_async_copy(own_ref, out_ref.at[x, z, c], own_sem)
    mine.start()
    mine.wait()
    for copy in first:
        copy.wait()
    second = []
    for k in range(NX - 1):
        second.append(remote(out_ref.at[:, z, c, :, left], out_ref.at[:, z, c, :, left], send.at[2, k], recv.at[2, k], zpeers[k]))
        second.append(remote(out_ref.at[x, :, c, :, right], out_ref.at[x, :, c, :, right], send.at[3, k], recv.at[3, k], xpeers[k]))
    for copy in second:
        copy.start()
    for copy in second:
        copy.wait()
    swap = remote(out_ref.at[:, :, c], out_ref.at[:, :, c], core_send, core_recv, twin)
    swap.start()
    swap.wait()


def gather(own, number):
    rows, cols = own.shape
    out = pl.pallas_call(
        gather_kernel,
        out_shape=jax.ShapeDtypeStruct((NX, NZ, NCORE, rows, cols), own.dtype),
        in_specs=[VMEM],
        out_specs=VMEM,
        scratch_shapes=[
            pltpu.SemaphoreType.DMA,
            pltpu.SemaphoreType.DMA((4, NX - 1)),
            pltpu.SemaphoreType.DMA((4, NX - 1)),
            pltpu.SemaphoreType.DMA,
            pltpu.SemaphoreType.DMA,
        ],
        compiler_params=pltpu.CompilerParams(collective_id=number, has_side_effects=True, vmem_limit_bytes=LIMIT),
        name="gather_rows",
    )(own)
    return out.reshape(PLANE * rows, cols)


def reduce_kernel(
    part_ref, gram_ref, rows_ref, out_gram_ref,
    from_twin, both, over_x, over_z, late_z, late_x, stage0, stage1, plane_sum, from_y,
    gram_in, gram_rows, gram_y,
    twin_send, twin_recv, send, recv, ysend, yrecv, gsend, grecv, gysend, gyrecv, bsend, brecv,
):
    me, x, z, c = place()
    y = lax.axis_index("grid")
    half = rows_ref.shape[1] // 2
    left, right = pl.ds(0, half), pl.ds(half, half)
    xs = [((x + k) % NX) for k in range(1, NX)]
    zs = [((z + k) % NZ) for k in range(1, NZ)]
    xpeers = [{"ens": v * NZ * NCORE + z * NCORE + c} for v in xs]
    zpeers = [{"ens": x * NZ * NCORE + v * NCORE + c} for v in zs]
    ypeers = [{"grid": (y + k) % NY} for k in range(1, NY)]
    twin = {"ens": me + 1 - 2 * c}
    greet_plane(me, ypeers)

    def gram_copy(k):
        peer = (me + k) % PLANE
        return remote(gram_ref.at[peer], gram_in.at[me], gsend.at[k], grecv.at[k], {"ens": peer})

    each(1, PLANE, lambda k: gram_copy(k).start())
    order = xs + [x]
    halves = [
        remote(part_ref.at[v, :, 1 - c], from_twin.at[v], twin_send.at[i], twin_recv.at[i], twin)
        for i, v in enumerate(order)
    ]
    for copy in halves:
        copy.start()
    x_first = []
    for i, v in enumerate(order):
        halves[i].wait()
        both[v] = part_ref[v, :, c] + from_twin[v]
        if i < NX - 1:
            copy = remote(both.at[v, :, :, left], over_x.at[i], send.at[0, i], recv.at[0, i], xpeers[i])
            copy.start()
            x_first.append(copy)
    z_first = []
    for i, v in enumerate(zs):
        copy = remote(both.at[:, v, :, right], over_z.at[i], send.at[1, i], recv.at[1, i], zpeers[i])
        copy.start()
        z_first.append(copy)
    gram_in[me] = gram_ref[me]
    each(1, PLANE, lambda k: gram_copy(k).wait())
    gram_rows[...] = jnp.sum(gram_in[...], axis=0)
    gram_over_y = [
        remote(gram_rows, gram_y.at[k], gysend.at[k], gyrecv.at[k], ypeers[k]) for k in range(NY - 1)
    ]
    for copy in gram_over_y:
        copy.start()
    for copy in gram_over_y:
        copy.wait()
    own_rows = gram_rows[...] + jnp.sum(gram_y[...], axis=0)
    out_gram_ref[me] = own_rows

    def gram_back(k):
        return remote(out_gram_ref.at[me], out_gram_ref.at[me], bsend.at[k], brecv.at[k], {"ens": (me + k) % PLANE})

    each(1, PLANE, lambda k: gram_back(k).start())
    for copy in x_first:
        copy.wait()
    stage0[...] = both[x, :, :, 0:half] + over_x[0] + over_x[1] + over_x[2]
    second = [
        remote(stage0.at[v], late_z.at[i], send.at[2, i], recv.at[2, i], zpeers[i]) for i, v in enumerate(zs)
    ]
    for copy in second:
        copy.start()
    for copy in z_first:
        copy.wait()
    stage1[...] = both[:, z, :, half:] + over_z[0] + over_z[1] + over_z[2]
    third = [
        remote(stage1.at[v], late_x.at[i], send.at[3, i], recv.at[3, i], xpeers[i]) for i, v in enumerate(xs)
    ]
    for copy in third:
        copy.start()
    for copy in second:
        copy.wait()
    plane_sum[:, 0:half] = stage0[z] + late_z[0] + late_z[1] + late_z[2]
    for copy in third:
        copy.wait()
    plane_sum[:, half:] = stage1[x] + late_x[0] + late_x[1] + late_x[2]
    over_y = [remote(plane_sum, from_y.at[k], ysend.at[k], yrecv.at[k], ypeers[k]) for k in range(NY - 1)]
    for copy in over_y:
        copy.start()
    for copy in over_y:
        copy.wait()
    rows_ref[...] = plane_sum[...] + from_y[0] + from_y[1] + from_y[2]
    each(1, PLANE, lambda k: gram_back(k).wait())


def reduce_sums(part, gram, number):
    total, cols = part.shape
    rows = total // PLANE
    half = cols // 2
    grows = gram.shape[0] // PLANE
    f32 = jnp.float32
    dma = pltpu.SemaphoreType.DMA
    out, summed = pl.pallas_call(
        reduce_kernel,
        out_shape=(
            jax.ShapeDtypeStruct((rows, cols), f32),
            jax.ShapeDtypeStruct((PLANE, grows, cols), f32),
        ),
        in_specs=[VMEM, VMEM],
        out_specs=(VMEM, VMEM),
        scratch_shapes=[
            pltpu.VMEM((NX, NZ, rows, cols), f32),
            pltpu.VMEM((NX, NZ, rows, cols), f32),
            pltpu.VMEM((NX - 1, NZ, rows, half), f32),
            pltpu.VMEM((NZ - 1, NX, rows, half), f32),
            pltpu.VMEM((NZ - 1, rows, half), f32),
            pltpu.VMEM((NX - 1, rows, half), f32),
            pltpu.VMEM((NZ, rows, half), f32),
            pltpu.VMEM((NX, rows, half), f32),
            pltpu.VMEM((rows, cols), f32),
            pltpu.VMEM((NY - 1, rows, cols), f32),
            pltpu.VMEM((PLANE, grows, cols), f32),
            pltpu.VMEM((grows, cols), f32),
            pltpu.VMEM((NY - 1, grows, cols), f32),
            dma((NX,)), dma((NX,)), dma((4, NX - 1)), dma((4, NX - 1)), dma((NY - 1,)), dma((NY - 1,)),
            dma((PLANE,)), dma((PLANE,)), dma((NY - 1,)), dma((NY - 1,)), dma((PLANE,)), dma((PLANE,)),
        ],
        compiler_params=pltpu.CompilerParams(collective_id=number, has_side_effects=True, vmem_limit_bytes=LIMIT),
        name="reduce_sums",
    )(part.reshape(NX, NZ, NCORE, rows, cols), gram.reshape(PLANE, grows, cols))
    return out, summed.reshape(gram.shape)


BLOCK = 64


def eliminated(m):
    size = m.shape[0]
    row = lax.broadcasted_iota(jnp.int32, m.shape, 0)
    col = lax.broadcasted_iota(jnp.int32, m.shape, 1)
    for j in range(0, size, 2):
        c0 = jnp.broadcast_to(m[:, j : j + 1], m.shape)
        c1 = jnp.broadcast_to(m[:, j + 1 : j + 2], m.shape)
        r0 = m[j : j + 1, :]
        r1 = m[j + 1 : j + 2, :]
        d0 = c0[j : j + 1, :]
        e = c0[j + 1 : j + 2, :]
        f = c1[j + 1 : j + 2, :]
        ratio = e / d0
        d1 = f - e * ratio
        u0 = r0 / d0
        u1 = (r1 - ratio * r0) / d1
        c1 = jnp.where(row > j + 1, c1 - c0 * ratio, 0.0)
        c0 = jnp.where(row > j, c0, 0.0)
        m = m - c0 * u0 - c1 * u1
    diag = jnp.sum(jnp.where(row == col, m, 0.0), axis=1, keepdims=True)
    return m * (1.0 / jnp.sqrt(diag))


def inverse_factor_kernel(gram_ref, out_ref, work):
    n = gram_ref.shape[0]
    work[:, 0:n] = gram_ref[...]
    row = lax.broadcasted_iota(jnp.int32, (n, n), 0)
    col = lax.broadcasted_iota(jnp.int32, (n, n), 1)
    work[:, n:] = jnp.where(row == col, 1.0, 0.0)
    brow = lax.broadcasted_iota(jnp.int32, (BLOCK, BLOCK), 0)
    bcol = lax.broadcasted_iota(jnp.int32, (BLOCK, BLOCK), 1)
    unit = jnp.where(brow == bcol, 1.0, 0.0)
    for low in range(0, n, BLOCK):
        high = low + BLOCK
        block = work[low:high, low:high]
        inv = eliminated(jnp.concatenate([block, unit], axis=1))[:, BLOCK:]
        scaled = jnp.dot(inv, work[low:high, :], precision=HIGHEST, preferred_element_type=jnp.float32)
        out_ref[low:high, :] = scaled[:, n:]
        if high < n:
            lower = scaled[:, high:n]
            update = lax.dot_general(
                lower, scaled, (((0,), (0,)), ((), ())), precision=HIGHEST, preferred_element_type=jnp.float32
            )
            work[high:, :] = work[high:, :] - update


def inverse_factor(gram):
    n = gram.shape[0]
    return pl.pallas_call(
        inverse_factor_kernel,
        out_shape=jax.ShapeDtypeStruct((n, n), jnp.float32),
        in_specs=[VMEM],
        out_specs=VMEM,
        scratch_shapes=[pltpu.VMEM((n, 2 * n), jnp.float32)],
        name="inverse_factor",
    )(gram)


def halos(block, width):
    count = lax.axis_size("grid")
    forward = [(i, i + 1) for i in range(count - 1)]
    backward = [(target, source) for source, target in forward]
    low = lax.ppermute(block[:, block.shape[1] - width :], "grid", forward)
    high = lax.ppermute(block[:, :width], "grid", backward)
    return jnp.concatenate([low, block, high], axis=1)


def localize(snapshots, tile_mask, kernels):
    diags = kernels.shape[0]
    half = diags // 2
    tile_width = kernels.shape[1]
    scen_dev = snapshots.shape[0]
    tiles_dev = tile_mask.shape[0]
    tiles = halos(snapshots, half * tile_width).reshape(scen_dev, tiles_dev + 2 * half, tile_width)
    total = jnp.zeros((scen_dev, tiles_dev, tile_width), jnp.float32)
    for diag in range(diags):
        prod = jnp.einsum(
            "sit,tu->siu",
            tiles[:, diag : diag + tiles_dev],
            kernels[diag],
            preferred_element_type=jnp.float32,
        )
        total = total + prod * tile_mask[:, diag].astype(jnp.float32)[None, :, None]
    return total.reshape(scen_dev, tiles_dev * tile_width)


def product(fields, span):
    high = span.astype(jnp.bfloat16)
    low = (span - high.astype(jnp.float32)).astype(jnp.bfloat16)
    both = jnp.dot(fields, jnp.concatenate([high, low], axis=1), preferred_element_type=jnp.float32)
    cols = span.shape[1]
    return both[:, :cols] + both[:, cols:]


def span_of(fields, mixing):
    return lax.dot_general(fields, mixing, (((0,), (0,)), ((), ())), preferred_element_type=jnp.float32)


def gram_of(span):
    return lax.dot_general(span, span, (((0,), (0,)), ((), ())), precision=HIGHEST)


def times_inverse_transposed(rows, inverse):
    return lax.dot_general(rows, inverse, (((1,), (1,)), ((), ())), precision=HIGHEST)


def per_device(snapshots, tile_mask, kernels, test_matrix):
    total_cells = snapshots.shape[1] * lax.axis_size("grid")
    rank_width = test_matrix.shape[1]
    mixing = gather(test_matrix, 1)
    total = localize(snapshots, tile_mask, kernels)
    block_means = jnp.mean(total, axis=0, keepdims=True)
    blocks, all_means = exchange(
        (total - block_means).astype(jnp.bfloat16), jnp.broadcast_to(block_means, (8, total.shape[1]))
    )
    all_means = all_means[:, :1]
    shift = all_means - jnp.mean(all_means, axis=0, keepdims=True)
    fields = (blocks.astype(jnp.float32) + shift).astype(jnp.bfloat16)
    fields = fields.reshape(-1, fields.shape[2])

    first_span = span_of(fields, mixing)
    rows, gram = reduce_sums(product(fields, first_span), gram_of(first_span), 2)
    weights = times_inverse_transposed(rows, inverse_factor(gram)).astype(jnp.bfloat16)
    second_span = span_of(fields, gather(weights, 3))
    rows, gram = reduce_sums(product(fields, second_span), gram_of(second_span), 4)
    inverse = inverse_factor(gram)
    basis = times_inverse_transposed(second_span, inverse) * math.sqrt(total_cells)
    coefficients = times_inverse_transposed(rows, inverse) * math.sqrt(rank_width / total_cells)
    return (basis, coefficients)


def solution(mesh):
    return jax.shard_map(
        per_device,
        mesh=mesh,
        in_specs=(P("ens", "grid"), P("grid", None), P(), P("ens", None)),
        out_specs=(P(("grid", "ens"), None), P("ens", None)),
        check_vma=False,
    )
```

time: 960 us -> 261 us (0.27)
  waiting for transfers between devices: 609 us -> 0.01 us
  Pallas kernels: 0 us -> 210 us
  blocking collectives: 148 us -> 0 us
  other arithmetic: 125 us -> 18.5 us
  between operations: 17.4 us -> 0.87 us
  local copies, waits for them, and re-layouts: 17.5 us -> 4.45 us
  matrix products: 33.6 us -> 22.2 us
    psum x3 -> x0, waiting for transfers between devices: 330 us -> none  [the longest x2 290 us: orthonormal(): gram = lax.psum(local_gram, ('grid', 'ens'))]
    pallas_call x0 -> x7, Pallas kernels: none -> 210 us  [the longest x2 90.1 us: reduce_sums(): pl.pallas_call(reduce_kernel, out_shape=(jax.ShapeDtypeStruct((rows, cols...]
    reduce_scatter x2 -> x0, waiting for transfers between devices: 180 us -> none  [scenario_span(): lax.psum_scatter(lax.dot_general(fields, mixing, (((0,), (0,)), ((), ()))...]
    psum x2 -> x0, blocking collectives: 148 us -> none  [the longest x1 130 us: per_device(): means = lax.psum(column, 'ens') / total_scen]
    another operation x18 -> x0, other arithmetic: 108 us -> none  [the longest x13 68.6 us: orthonormal(): lower = jnp.linalg.cholesky(gram)]
    all_gather x2 -> x0, waiting for transfers between devices: 92.3 us -> none  [scenario_weights(): lax.all_gather(basis_half, 'ens', axis=0, tiled=True)]
    dot_general x6 -> x9, matrix products: 21.8 us -> 14.6 us  [the longest x3 6.37 us: times_inverse_transposed(): lax.dot_general(rows, inverse, (((1,), (1,)), ((), ())), precision=HIGHEST)]
  transfers between devices with their start and end apart: 9 -> 2, of which waited for: 9 -> 0; matrix products, arithmetic and copies ran while one was open for 0% -> 0% of each run, Pallas kernels for 0% -> 8%
where the time goes in v1:
time: 261 us
  Pallas kernels  210 us (80%)
  matrix products  22.2 us (9%)
  other arithmetic  18.5 us (7%)
  starting transfers between devices  4.9 us (2%)
  local copies, waits for them, and re-layouts  4.45 us (2%)
    pallas_call x2, Pallas kernels, reduce_sums(): pl.pallas_call(reduce_kernel, out_shape=(jax.ShapeDtypeStruct((rows, cols...  90.1 us
    pallas_call x1, Pallas kernels, exchange(): pl.pallas_call(exchange_kernel, out_shape=(jax.ShapeDtypeStruct((PLANE, s...  47.3 us
    pallas_call x2, Pallas kernels, gather(): pl.pallas_call(gather_kernel, out_shape=jax.ShapeDtypeStruct((NX, NZ, NCO...  38.1 us
    pallas_call x2, Pallas kernels, inverse_factor(): pl.pallas_call(inverse_factor_kernel, out_shape=jax.ShapeDtypeStruct((n,...  34.4 us
    concatenate x1, other arithmetic, halos(): return jnp.concatenate([low, block, high], axis=1)  7.68 us
    dot_general x5, matrix products, localize(): jnp.einsum('sit,tu->siu', tiles[:, diag:diag + tiles_dev], kernels[diag],...  7.53 us
    dot_general x3, matrix products, times_inverse_transposed(): lax.dot_general(rows, inverse, (((1,), (1,)), ((), ())), precision=HIGHEST)  6.37 us
  transfers between devices with their start and end apart: 2, of which 0 were waited for; matrix products, arithmetic and copies ran while one was open for 0% of the time, Pallas kernels for 8%

profile of v1, /device:TPU:0, one launch (start us, length us, event | category | flops | bytes accessed | tf_op | source)
XLA Modules:
  0.0 260.8 jit_solution(3790191831901788227)
XLA Ops:
  0.6 3.2 %copy.7 = bf16[128,8192]{0,1:T(8,128)(2,1)S(1)} copy(bf16[128,8192]{1,0:T(8,128)(2,1)} %param.4) | data formatting | bytes 4194304 | tf_op args[0]
  3.9 3.6 %collective-permute-start = (bf16[128,1024]{0,1:T(8,128)(2,1)S(1)}, bf16[128,1024]{0,1:T(8,128)(2,1)S(1)}, u32[]{:S(2)}, u32[]{:S(2)}) collective-permute-start(bf16[128,1024]{0,1:T(8,128)(2,1)S(1)} %get-tuple-element.18), channel_id=1, source_target_pairs={{0,32},{32,64},{64,96},{1,33},{33,65},{65,97},{2,34},{34,66},{66,9... | collective-permute-start | bytes 786440 | tf_op jit(solution)/shard_map/ppermute | solution.py:362
  7.5 1.3 collective-permute-start.1
  8.8 20.7 %gather_rows.2 = bf16[4,4,2,128,256]{4,3,2,1,0:T(8,128)(2,1)} custom-call(bf16[128,256]{1,0:T(8,128)(2,1)} %own_ref.1), custom_call_target="tpu_custom_call" | custom-call | tf_op jit(solution)/shard_map/gather_rows/pallas_call | solution.py:150
  29.6 7.7 %pad_maximum_fusion = bf16[128,10240]{0,1:T(8,128)(2,1)S(1)} fusion(bf16[128,1024]{0,1:T(8,128)(2,1)S(1)} %collective-permute-done.1, bf16[128,8192]{0,1:T(8,128)(2,1)S(1)} %copy.7, bf16[128,1024]{0,1:T(8,128)(2,1)S(1)} %collective-permute-done), kind=kLoop, calls=%fused_computation.5 | loop fusion | flops 7864320 | bytes 5242880 | tf_op jit(solution)/shard_map/concatenate | solution.py:364
  38.6 1.3 fusion.3
  39.9 1.3 fusion.5
  41.2 1.3 fusion.7
  42.5 2.4 fusion.25
  45.4 1.7 subtract_convert_fusion.local_ref
  47.7 47.3 %exchange.1 = (bf16[32,128,256]{2,1,0:T(8,128)(2,1)}, f32[32,8,256]{2,1,0:T(8,128)}) custom-call(bf16[128,8192]{1,0:T(8,128)(2,1)} %subtract_convert_fusion.local_ref, f32[8,8192]{1,0:T(8,128)} %broadcast_in_dim.2.means_ref), custom_call_target="tpu_custom_call" | custom-call | tf_op jit(solution)/shard_map/exchange/pallas_call | solution.py:100
  97.2 2.1 add_convert_fusion
  100.2 1.3 fusion.14
  101.5 2.5 slice_add_fusion.1
  105.1 50.7 %reduce_sums.2 = (f32[128,256]{1,0:T(8,128)}, f32[32,8,256]{2,1,0:T(8,128)}) custom-call(f32[4,4,2,128,256]{4,3,2,1,0:T(8,128)} %bitcast.82, f32[32,8,256]{2,1,0:T(8,128)} %convolution_bitcast_fusion.1.gram_ref), custom_call_target="tpu_custom_call" | custom-call | tf_op jit(solution)/shard_map/reduce_sums/pallas_call | solution.py:266
  155.8 17.2 %inverse_factor.2 = f32[256,256]{1,0:T(8,128)} custom-call(f32[256,256]{1,0:T(8,128)} %bitcast.90), custom_call_target="tpu_custom_call" | custom-call | tf_op jit(solution)/shard_map/inverse_factor/pallas_call | solution.py:348
  173.0 2.0 convolution_convert_fusion.own_ref
  175.1 17.3 %gather_rows.3 = bf16[4,4,2,128,256]{4,3,2,1,0:T(8,128)(2,1)} custom-call(bf16[128,256]{1,0:T(8,128)(2,1)} %convolution_convert_fusion.own_ref), custom_call_target="tpu_custom_call" | custom-call | tf_op jit(solution)/shard_map/gather_rows/pallas_call | solution.py:150
  192.4 2.5 subtract_convert_fusion.1
  196.2 2.5 slice_add_fusion
  199.8 39.4 %reduce_sums.3 = (f32[128,256]{1,0:T(8,128)}, f32[32,8,256]{2,1,0:T(8,128)}) custom-call(f32[4,4,2,128,256]{4,3,2,1,0:T(8,128)} %bitcast.83, f32[32,8,256]{2,1,0:T(8,128)} %convolution_bitcast_fusion.gram_ref), custom_call_target="tpu_custom_call" | custom-call | tf_op jit(solution)/shard_map/reduce_sums/pallas_call | solution.py:266
  239.3 17.2 %inverse_factor.3 = f32[256,256]{1,0:T(8,128)} custom-call(f32[256,256]{1,0:T(8,128)} %bitcast.91), custom_call_target="tpu_custom_call" | custom-call | tf_op jit(solution)/shard_map/inverse_factor/pallas_call | solution.py:348
  256.5 2.2 convolution_multiply_fusion
  258.7 2.1 convolution_multiply_fusion.1
  (23 shorter events, 9.1 us)
Async XLA Ops:
  3.9 25.7 %copy-start.2 = (s32[16,5]{0,1:T(8,128)S(1)}, s32[16,5]{0,1:T(8,128)}, u32[]{:S(2)}) copy-start(s32[16,5]{0,1:T(8,128)} %param.5) | copy-start | bytes 964
  3.9 25.7 %collective-permute-start = (bf16[128,1024]{0,1:T(8,128)(2,1)S(1)}, bf16[128,1024]{0,1:T(8,128)(2,1)S(1)}, u32[]{:S(2)}, u32[]{:S(2)}) collective-permute-start(bf16[128,1024]{0,1:T(8,128)(2,1)S(1)} %get-tuple-element.18), channel_id=1, source_target_pairs={{0,32},{32,64},{64,96},{1,33},{33,65},{65,97},{2,34},{34,66},{66,9... | collective-permute-start | bytes 786440 | tf_op jit(solution)/shard_map/ppermute | solution.py:362
  7.5 22.1 %collective-permute-start.1 = (bf16[128,1024]{0,1:T(8,128)(2,1)S(1)}, bf16[128,1024]{0,1:T(8,128)(2,1)S(1)}, u32[]{:S(2)}, u32[]{:S(2)}) collective-permute-start(bf16[128,1024]{0,1:T(8,128)(2,1)S(1)} %get-tuple-element.19), channel_id=1, source_target_pairs={{32,0},{64,32},{96,64},{33,1},{65,33},{97,65},{34,2},{66,34},{98,6... | collective-permute-start | bytes 786440 | tf_op jit(solution)/shard_map/ppermute | solution.py:363
  29.6 7.7 %copy-start = (bf16[5,512,512]{2,1,0:T(8,128)(2,1)S(1)}, bf16[5,512,512]{2,1,0:T(8,128)(2,1)}, u32[]{:S(2)}) copy-start(bf16[5,512,512]{2,1,0:T(8,128)(2,1)} %param.6) | copy-start | bytes 7864324
  95.0 4.3 %copy-start.1 = (bf16[4,4,2,128,256]{4,3,2,1,0:T(8,128)(2,1)S(1)}, bf16[4,4,2,128,256]{4,3,2,1,0:T(8,128)(2,1)}, u32[]{:S(2)}) copy-start(bf16[4,4,2,128,256]{4,3,2,1,0:T(8,128)(2,1)} %gather_rows.2) | copy-start | bytes 6291460

commit v2 on v1

--- a/solution.py
+++ b/solution.py
@@ -57,30 +57,100 @@
     lax.fori_loop(low, high, step, 0)
 
 
-def exchange_kernel(local_ref, means_ref, out_ref, all_means_ref, own_sem, send, recv, msend, mrecv):
-    me = lax.axis_index("ens")
+def spread_kernel(
+    snap_ref, mask_ref, kernels_ref, mix_ref,
+    out_ref, all_means_ref, mixing_ref,
+    padded, blocks, means,
+    load_sem, own_sem, hsend, hrecv, send, recv, msend, mrecv, tsend, trecv, twin_send, twin_recv,
+):
+    me, x, z, c = place()
+    y = lax.axis_index("grid")
+    chip = me // NCORE
+    diags, tile, _ = kernels_ref.shape
+    halo = (diags // 2) * tile
+    scen, cells = snap_ref.shape
+    tiles = cells // tile
     width = out_ref.shape[2]
-    greet_plane(me)
-
-    def columns(owner):
-        return pl.ds(pl.multiple_of(owner * width, width), width)
-
-    def copies(k):
-        peer = {"ens": (me + k) % PLANE}
-        cols = columns((me + k) % PLANE)
+    inner = tiles - 2 * (diags // 2)
+    up, down = {"grid": (y + 1) % NY}, {"grid": (y + NY - 1) % NY}
+    greet_plane(me, (up, down))
+
+    load = pltpu.make_async_copy(snap_ref, padded.at[:, pl.ds(halo, cells)], load_sem)
+    load.start()
+    over_y = (
+        remote(snap_ref.at[:, pl.ds(cells - halo, halo)], padded.at[:, pl.ds(0, halo)], hsend.at[0], hrecv.at[0], up),
+        remote(snap_ref.at[:, pl.ds(0, halo)], padded.at[:, pl.ds(halo + cells, halo)], hsend.at[1], hrecv.at[1], down),
+    )
+    for copy in over_y:
+        copy.start()
+
+    half = mix_ref.shape[1] // 2
+    left, right = pl.ds(0, half), pl.ds(half, half)
+    xpeers = [{"ens": ((x + k) % NX) * NZ * NCORE + z * NCORE + c} for k in range(1, NX)]
+    zpeers = [{"ens": x * NZ * NCORE + ((z + k) % NZ) * NCORE + c} for k in range(1, NZ)]
+    twin = {"ens": me + 1 - 2 * c}
+    first, second = [], []
+    for k in range(NX - 1):
+        first.append(remote(mix_ref.at[:, left], mixing_ref.at[x, z, c, :, left], tsend.at[0, k], trecv.at[0, k], xpeers[k]))
+        first.append(remote(mix_ref.at[:, right], mixing_ref.at[x, z, c, :, right], tsend.at[1, k], trecv.at[1, k], zpeers[k]))
+        second.append(remote(mixing_ref.at[:, z, c, :, left], mixing_ref.at[:, z, c, :, left], tsend.at[2, k], trecv.at[2, k], zpeers[k]))
+        second.append(remote(mixing_ref.at[x, :, c, :, right], mixing_ref.at[x, :, c, :, right], tsend.at[3, k], trecv.at[3, k], xpeers[k]))
+    swap = remote(mixing_ref.at[:, :, c], mixing_ref.at[:, :, c], twin_send, twin_recv, twin)
+    for copy in first:
+        copy.start()
+    mine = pltpu.make_async_copy(mix_ref, mixing_ref.at[x, z, c], own_sem.at[0])
+    mine.start()
+    mine.wait()
+    load.wait()
+
+    def copies(i, core):
+        owner = NCORE * i + core
+        cols = pl.ds(core * width, width)
         return (
-            remote(means_ref.at[:, cols], all_means_ref.at[me], msend.at[k], mrecv.at[k], peer),
-            remote(local_ref.at[:, cols], out_ref.at[me], send.at[k], recv.at[k], peer),
+            remote(means.at[i, :, cols], all_means_ref.at[me], msend.at[owner], mrecv.at[me], {"ens": owner}),
+            remote(blocks.at[i, :, cols], out_ref.at[me], send.at[owner], recv.at[me], {"ens": owner}),
         )
 
-    def start(k):
-        for copy in copies(k):
-            copy.start()
-
-    each(1, PLANE, start)
+    def localize(i):
+        total = jnp.zeros((scen, tile), jnp.float32)
+        for diag in range(diags):
+            start = pl.multiple_of((i + diag) * tile, tile)
+            prod = jnp.dot(padded[:, pl.ds(start, tile)], kernels_ref[diag], preferred_element_type=jnp.float32)
+            total = total + prod * mask_ref[i, diag].astype(jnp.float32)
+        mean = jnp.mean(total, axis=0, keepdims=True)
+        means[i] = jnp.broadcast_to(mean, (8, tile))
+        blocks[i] = (total - mean).astype(blocks.dtype)
+        for core in range(NCORE):
+
+            @pl.when(NCORE * i + core != me)
+            def _():
+                for copy in copies(i, core):
+                    copy.start()
+
+    each(0, inner, lambda n: localize(diags // 2 + (chip + 5 * n) % inner))
+    for copy in first:
+        copy.wait()
+    for copy in second:
+        copy.start()
+    for copy in over_y:
+        copy.wait()
+
+    @pl.when(y == 0)
+    def _():
+        padded[:, 0:halo] = jnp.zeros((scen, halo), padded.dtype)
+
+    @pl.when(y == NY - 1)
+    def _():
+        padded[:, halo + cells :] = jnp.zeros((scen, halo), padded.dtype)
+
+    each(0, tiles - inner, lambda n: localize((inner + diags // 2 + (chip + n) % (tiles - inner)) % tiles))
+    for copy in second:
+        copy.wait()
+    swap.start()
+
     own = (
-        pltpu.make_async_copy(local_ref.at[:, columns(me)], out_ref.at[me], own_sem.at[0]),
-        pltpu.make_async_copy(means_ref.at[:, columns(me)], all_means_ref.at[me], own_sem.at[1]),
+        pltpu.make_async_copy(blocks.at[chip, :, pl.ds(pl.multiple_of(c * width, width), width)], out_ref.at[me], own_sem.at[0]),
+        pltpu.make_async_copy(means.at[chip, :, pl.ds(pl.multiple_of(c * width, width), width)], all_means_ref.at[me], own_sem.at[1]),
     )
     for copy in own:
         copy.start()
@@ -88,27 +158,43 @@
         copy.wait()
 
     def finish(k):
-        for copy in copies(k):
-            copy.wait()
+        source = (me + k) % PLANE
+        target = (me + PLANE - k) % PLANE
+        tile_of, cols = target // NCORE, pl.ds(pl.multiple_of((target % NCORE) * width, width), width)
+        remote(means.at[tile_of, :, cols], all_means_ref.at[source], msend.at[target], mrecv.at[source], {"ens": target}).wait()
+        remote(blocks.at[tile_of, :, cols], out_ref.at[source], send.at[target], recv.at[source], {"ens": target}).wait()
 
     each(1, PLANE, finish)
-
-
-def exchange(local, means):
-    scen, cells = local.shape
+    swap.wait()
+
+
+def spread(snapshots, tile_mask, kernels, mix):
+    scen, cells = snapshots.shape
+    diags, tile, _ = kernels.shape
+    tiles = cells // tile
+    halo = (diags // 2) * tile
     width = cells // PLANE
+    dma = pltpu.SemaphoreType.DMA
     return pl.pallas_call(
-        exchange_kernel,
+        spread_kernel,
         out_shape=(
-            jax.ShapeDtypeStruct((PLANE, scen, width), local.dtype),
-            jax.ShapeDtypeStruct((PLANE, means.shape[0], width), means.dtype),
+            jax.ShapeDtypeStruct((PLANE, scen, width), jnp.bfloat16),
+            jax.ShapeDtypeStruct((PLANE, 8, width), jnp.float32),
+            jax.ShapeDtypeStruct((NX, NZ, NCORE) + mix.shape, mix.dtype),
         ),
-        in_specs=[VMEM, VMEM],
-        out_specs=(VMEM, VMEM),
-        scratch_shapes=[pltpu.SemaphoreType.DMA((2,))] + [pltpu.SemaphoreType.DMA((PLANE,))] * 4,
+        in_specs=[ANY, pl.BlockSpec(memory_space=pltpu.SMEM), VMEM, VMEM],
+        out_specs=(VMEM, VMEM, VMEM),
+        scratch_shapes=[
+            pltpu.VMEM((scen, cells + 2 * halo), jnp.bfloat16),
+            pltpu.VMEM((tiles, scen, tile), jnp.bfloat16),
+            pltpu.VMEM((tiles, 8, tile), jnp.float32),
+            dma, dma((2,)), dma((2,)), dma((2,)),
+            dma((PLANE,)), dma((PLANE,)), dma((PLANE,)), dma((PLANE,)),
+            dma((4, NX - 1)), dma((4, NX - 1)), dma, dma,
+        ],
         compiler_params=pltpu.CompilerParams(collective_id=0, has_side_effects=True, vmem_limit_bytes=LIMIT),
-        name="exchange",
-    )(local, means)
+        name="spread",
+    )(snapshots, tile_mask, kernels, mix)
 
 
 def gather_kernel(own_ref, out_ref, own_sem, send, recv, core_send, core_recv):
@@ -355,34 +441,6 @@
     )(gram)
 
 
-def halos(block, width):
-    count = lax.axis_size("grid")
-    forward = [(i, i + 1) for i in range(count - 1)]
-    backward = [(target, source) for source, target in forward]
-    low = lax.ppermute(block[:, block.shape[1] - width :], "grid", forward)
-    high = lax.ppermute(block[:, :width], "grid", backward)
-    return jnp.concatenate([low, block, high], axis=1)
-
-
-def localize(snapshots, tile_mask, kernels):
-    diags = kernels.shape[0]
-    half = diags // 2
-    tile_width = kernels.shape[1]
-    scen_dev = snapshots.shape[0]
-    tiles_dev = tile_mask.shape[0]
-    tiles = halos(snapshots, half * tile_width).reshape(scen_dev, tiles_dev + 2 * half, tile_width)
-    total = jnp.zeros((scen_dev, tiles_dev, tile_width), jnp.float32)
-    for diag in range(diags):
-        prod = jnp.einsum(
-            "sit,tu->siu",
-            tiles[:, diag : diag + tiles_dev],
-            kernels[diag],
-            preferred_element_type=jnp.float32,
-        )
-        total = total + prod * tile_mask[:, diag].astype(jnp.float32)[None, :, None]
-    return total.reshape(scen_dev, tiles_dev * tile_width)
-
-
 def product(fields, span):
     high = span.astype(jnp.bfloat16)
     low = (span - high.astype(jnp.float32)).astype(jnp.bfloat16)
@@ -406,12 +464,8 @@
 def per_device(snapshots, tile_mask, kernels, test_matrix):
     total_cells = snapshots.shape[1] * lax.axis_size("grid")
     rank_width = test_matrix.shape[1]
-    mixing = gather(test_matrix, 1)
-    total = localize(snapshots, tile_mask, kernels)
-    block_means = jnp.mean(total, axis=0, keepdims=True)
-    blocks, all_means = exchange(
-        (total - block_means).astype(jnp.bfloat16), jnp.broadcast_to(block_means, (8, total.shape[1]))
-    )
+    blocks, all_means, mixing = spread(snapshots, tile_mask, kernels, test_matrix)
+    mixing = mixing.reshape(-1, rank_width)
     all_means = all_means[:, :1]
     shift = all_means - jnp.mean(all_means, axis=0, keepdims=True)
     fields = (blocks.astype(jnp.float32) + shift).astype(jnp.bfloat16)

time: 261 us -> 222 us (0.85)
  Pallas kernels: 210 us -> 196 us
  other arithmetic: 18.5 us -> 9.18 us
  matrix products: 22.2 us -> 14.6 us
  starting transfers between devices: 4.9 us -> 0 us
  local copies, waits for them, and re-layouts: 4.45 us -> 1.37 us
    pallas_call x2 -> x1, Pallas kernels: 38.1 us -> 18 us  [gather(): pl.pallas_call(gather_kernel, out_shape=jax.ShapeDtypeStruct((NX, NZ, NCO...]
    pallas_call x1, Pallas kernels: 47.3 us -> 58 us  [spread(): pl.pallas_call(spread_kernel, out_shape=(jax.ShapeDtypeStruct((PLANE, sce...]
    concatenate x1 -> x0, other arithmetic: 7.68 us -> none  [halos(): return jnp.concatenate([low, block, high], axis=1)]
    dot_general x5 -> x0, matrix products: 7.53 us -> none  [localize(): jnp.einsum('sit,tu->siu', tiles[:, diag:diag + tiles_dev], kernels[diag],...]
    ppermute x2 -> x0, starting transfers between devices: 4.9 us -> none  [the longest x1 3.61 us: halos(): low = lax.ppermute(block[:, block.shape[1] - width:], 'grid', forward)]
    pallas_call x2, Pallas kernels: 90.1 us -> 85.3 us  [reduce_sums(): pl.pallas_call(reduce_kernel, out_shape=(jax.ShapeDtypeStruct((rows, cols...]
  transfers between devices with their start and end apart: 2 -> 0, of which waited for: 0 -> 0; matrix products, arithmetic and copies ran while one was open for 0% -> 0% of each run, Pallas kernels for 8% -> 0%
where the time goes in v2:
time: 222 us
  Pallas kernels  196 us (88%)
  matrix products  14.6 us (7%)
  other arithmetic  9.18 us (4%)
    pallas_call x2, Pallas kernels, reduce_sums(): pl.pallas_call(reduce_kernel, out_shape=(jax.ShapeDtypeStruct((rows, cols...  85.3 us
    pallas_call x1, Pallas kernels, spread(): pl.pallas_call(spread_kernel, out_shape=(jax.ShapeDtypeStruct((PLANE, sce...  58 us
    pallas_call x2, Pallas kernels, inverse_factor(): pl.pallas_call(inverse_factor_kernel, out_shape=jax.ShapeDtypeStruct((n,...  34.4 us
    pallas_call x1, Pallas kernels, gather(): pl.pallas_call(gather_kernel, out_shape=jax.ShapeDtypeStruct((NX, NZ, NCO...  18 us
    dot_general x3, matrix products, times_inverse_transposed(): lax.dot_general(rows, inverse, (((1,), (1,)), ((), ())), precision=HIGHEST)  6.37 us
    add x2, other arithmetic, product(): return both[:, :cols] + both[:, cols:]  4.96 us

profile of v2, /device:TPU:0, one launch (start us, length us, event | category | flops | bytes accessed | tf_op | source)
XLA Modules:
  0.0 221.6 jit_solution(7529203513426092230)
XLA Ops:
  0.6 1.4 copy.6.mask_ref
  2.0 58.0 %spread.1 = (bf16[32,128,256]{2,1,0:T(8,128)(2,1)}, f32[32,8,256]{2,1,0:T(8,128)}, bf16[4,4,2,128,256]{4,3,2,1,0:T(8,128)(2,1)}) custom-call(bf16[128,8192]{1,0:T(8,128)(2,1)} %snap_ref.1, s32[16,5]{1,0:T(8,128)} %copy.6.mask_ref, bf16[5,512,512]{2,1,0:T(8,128)(2,1)} %kernels_ref.1, bf16[128,256]{1,0:T(8,128)(2,1)} %mix_ref.1), custom_call_target="tpu_custom_call" | custom-call | tf_op jit(solution)/shard_map/spread/pallas_call | solution.py:178
  60.0 1.0 slice_reduce_fusion
  61.0 1.0 slice_subtract_fusion
  62.0 0.0 copy-start
  62.0 2.2 %add_convert_fusion = bf16[32,128,256]{2,1,0:T(8,128)(2,1)S(1)} fusion(bf16[32,128,256]{2,1,0:T(8,128)(2,1)} %get-tuple-element.9, f32[32,256]{1,0:T(8,128)S(1)} %bitcast.39), kind=kLoop, calls=%fused_computation.2 | loop fusion | flops 3145728 | bytes 4227072 | tf_op jit(solution)/shard_map/convert_element_type | solution.py:471
  64.3 0.0 copy-done
  64.3 1.0 subtract_convert_fusion.1
  65.2 1.1 convolution_bitcast_fusion.1.gram_ref
  66.4 1.3 fusion
  67.6 2.5 %slice_add_fusion.1 = f32[4096,256]{1,0:T(8,128)} fusion(f32[4096,512]{1,0:T(8,128)S(1)} %fusion), kind=kLoop, calls=%fused_computation.1 | loop fusion | flops 1048576 | bytes 12582912 | tf_op jit(solution)/shard_map/add | solution.py:449
  70.1 45.5 %reduce_sums.2 = (f32[128,256]{1,0:T(8,128)}, f32[32,8,256]{2,1,0:T(8,128)}) custom-call(f32[4,4,2,128,256]{4,3,2,1,0:T(8,128)} %bitcast.34, f32[32,8,256]{2,1,0:T(8,128)} %convolution_bitcast_fusion.1.gram_ref), custom_call_target="tpu_custom_call" | custom-call | tf_op jit(solution)/shard_map/reduce_sums/pallas_call | solution.py:352
  115.6 17.2 %inverse_factor.2 = f32[256,256]{1,0:T(8,128)} custom-call(f32[256,256]{1,0:T(8,128)} %bitcast.37), custom_call_target="tpu_custom_call" | custom-call | tf_op jit(solution)/shard_map/inverse_factor/pallas_call | solution.py:434
  132.8 2.0 convolution_convert_fusion.own_ref
  134.9 18.0 %gather_rows.1 = bf16[4,4,2,128,256]{4,3,2,1,0:T(8,128)(2,1)} custom-call(bf16[128,256]{1,0:T(8,128)(2,1)} %convolution_convert_fusion.own_ref), custom_call_target="tpu_custom_call" | custom-call | tf_op jit(solution)/shard_map/gather_rows/pallas_call | solution.py:236
  152.9 2.5 %subtract_convert_fusion = (bf16[256,256]{0,1:T(8,128)(2,1)S(1)}, bf16[256,256]{0,1:T(8,128)(2,1)S(1)}, f32[256,256]{0,1:T(8,128)S(1)}) fusion(bf16[4096,256]{1,0:T(8,128)(2,1)S(1)} %bitcast.32, bf16[4096,256]{1,0:T(8,128)(2,1)} %bitcast.36), kind=kOutput, calls=%fused_computation.16 | convolution fusion | flops 537133056 | bytes 4718592 | tf_op jit(solution)/shard_map/dot_general | solution.py:453
  155.4 1.1 convolution_bitcast_fusion.gram_ref
  156.5 1.3 fusion.4
  157.8 2.5 %slice_add_fusion = f32[4096,256]{1,0:T(8,128)} fusion(f32[4096,512]{1,0:T(8,128)S(1)} %fusion.4), kind=kLoop, calls=%fused_computation | loop fusion | flops 1048576 | bytes 12582912 | tf_op jit(solution)/shard_map/add | solution.py:449
  160.3 39.8 %reduce_sums.3 = (f32[128,256]{1,0:T(8,128)}, f32[32,8,256]{2,1,0:T(8,128)}) custom-call(f32[4,4,2,128,256]{4,3,2,1,0:T(8,128)} %bitcast.35, f32[32,8,256]{2,1,0:T(8,128)} %convolution_bitcast_fusion.gram_ref), custom_call_target="tpu_custom_call" | custom-call | tf_op jit(solution)/shard_map/reduce_sums/pallas_call | solution.py:352
  200.1 17.2 %inverse_factor.3 = f32[256,256]{1,0:T(8,128)} custom-call(f32[256,256]{1,0:T(8,128)} %bitcast.38), custom_call_target="tpu_custom_call" | custom-call | tf_op jit(solution)/shard_map/inverse_factor/pallas_call | solution.py:434
  217.3 2.1 convolution_multiply_fusion.1
  219.4 2.2 %convolution_multiply_fusion = f32[256,256]{1,0:T(8,128)} fusion(f32[256,256]{0,1:T(8,128)S(1)} %get-tuple-element.21, f32[256,256]{1,0:T(8,128)} %inverse_factor.3), kind=kOutput, calls=%fused_computation.3 | convolution fusion | flops 201392128 | bytes 786432 | tf_op jit(solution)/shard_map/dot_general | solution.py:461
  (2 shorter events, 0.0 us)
Async XLA Ops:
  62.0 2.3 %copy-start = (bf16[4,4,2,128,256]{4,3,2,1,0:T(8,128)(2,1)S(1)}, bf16[4,4,2,128,256]{4,3,2,1,0:T(8,128)(2,1)}, u32[]{:S(2)}) copy-start(bf16[4,4,2,128,256]{4,3,2,1,0:T(8,128)(2,1)} %get-tuple-element.11) | copy-start | bytes 6291460

commit v3 on v2

--- a/solution.py
+++ b/solution.py
@@ -251,135 +251,6 @@
     return out.reshape(PLANE * rows, cols)
 
 
-def reduce_kernel(
-    part_ref, gram_ref, rows_ref, out_gram_ref,
-    from_twin, both, over_x, over_z, late_z, late_x, stage0, stage1, plane_sum, from_y,
-    gram_in, gram_rows, gram_y,
-    twin_send, twin_recv, send, recv, ysend, yrecv, gsend, grecv, gysend, gyrecv, bsend, brecv,
-):
-    me, x, z, c = place()
-    y = lax.axis_index("grid")
-    half = rows_ref.shape[1] // 2
-    left, right = pl.ds(0, half), pl.ds(half, half)
-    xs = [((x + k) % NX) for k in range(1, NX)]
-    zs = [((z + k) % NZ) for k in range(1, NZ)]
-    xpeers = [{"ens": v * NZ * NCORE + z * NCORE + c} for v in xs]
-    zpeers = [{"ens": x * NZ * NCORE + v * NCORE + c} for v in zs]
-    ypeers = [{"grid": (y + k) % NY} for k in range(1, NY)]
-    twin = {"ens": me + 1 - 2 * c}
-    greet_plane(me, ypeers)
-
-    def gram_copy(k):
-        peer = (me + k) % PLANE
-        return remote(gram_ref.at[peer], gram_in.at[me], gsend.at[k], grecv.at[k], {"ens": peer})
-
-    each(1, PLANE, lambda k: gram_copy(k).start())
-    order = xs + [x]
-    halves = [
-        remote(part_ref.at[v, :, 1 - c], from_twin.at[v], twin_send.at[i], twin_recv.at[i], twin)
-        for i, v in enumerate(order)
-    ]
-    for copy in halves:
-        copy.start()
-    x_first = []
-    for i, v in enumerate(order):
-        halves[i].wait()
-        both[v] = part_ref[v, :, c] + from_twin[v]
-        if i < NX - 1:
-            copy = remote(both.at[v, :, :, left], over_x.at[i], send.at[0, i], recv.at[0, i], xpeers[i])
-            copy.start()
-            x_first.append(copy)
-    z_first = []
-    for i, v in enumerate(zs):
-        copy = remote(both.at[:, v, :, right], over_z.at[i], send.at[1, i], recv.at[1, i], zpeers[i])
-        copy.start()
-        z_first.append(copy)
-    gram_in[me] = gram_ref[me]
-    each(1, PLANE, lambda k: gram_copy(k).wait())
-    gram_rows[...] = jnp.sum(gram_in[...], axis=0)
-    gram_over_y = [
-        remote(gram_rows, gram_y.at[k], gysend.at[k], gyrecv.at[k], ypeers[k]) for k in range(NY - 1)
-    ]
-    for copy in gram_over_y:
-        copy.start()
-    for copy in gram_over_y:
-        copy.wait()
-    own_rows = gram_rows[...] + jnp.sum(gram_y[...], axis=0)
-    out_gram_ref[me] = own_rows
-
-    def gram_back(k):
-        return remote(out_gram_ref.at[me], out_gram_ref.at[me], bsend.at[k], brecv.at[k], {"ens": (me + k) % PLANE})
-
-    each(1, PLANE, lambda k: gram_back(k).start())
-    for copy in x_first:
-        copy.wait()
-    stage0[...] = both[x, :, :, 0:half] + over_x[0] + over_x[1] + over_x[2]
-    second = [
-        remote(stage0.at[v], late_z.at[i], send.at[2, i], recv.at[2, i], zpeers[i]) for i, v in enumerate(zs)
-    ]
-    for copy in second:
-        copy.start()
-    for copy in z_first:
-        copy.wait()
-    stage1[...] = both[:, z, :, half:] + over_z[0] + over_z[1] + over_z[2]
-    third = [
-        remote(stage1.at[v], late_x.at[i], send.at[3, i], recv.at[3, i], xpeers[i]) for i, v in enumerate(xs)
-    ]
-    for copy in third:
-        copy.start()
-    for copy in second:
-        copy.wait()
-    plane_sum[:, 0:half] = stage0[z] + late_z[0] + late_z[1] + late_z[2]
-    for copy in third:
-        copy.wait()
-    plane_sum[:, half:] = stage1[x] + late_x[0] + late_x[1] + late_x[2]
-    over_y = [remote(plane_sum, from_y.at[k], ysend.at[k], yrecv.at[k], ypeers[k]) for k in range(NY - 1)]
-    for copy in over_y:
-        copy.start()
-    for copy in over_y:
-        copy.wait()
-    rows_ref[...] = plane_sum[...] + from_y[0] + from_y[1] + from_y[2]
-    each(1, PLANE, lambda k: gram_back(k).wait())
-
-
-def reduce_sums(part, gram, number):
-    total, cols = part.shape
-    rows = total // PLANE
-    half = cols // 2
-    grows = gram.shape[0] // PLANE
-    f32 = jnp.float32
-    dma = pltpu.SemaphoreType.DMA
-    out, summed = pl.pallas_call(
-        reduce_kernel,
-        out_shape=(
-            jax.ShapeDtypeStruct((rows, cols), f32),
-            jax.ShapeDtypeStruct((PLANE, grows, cols), f32),
-        ),
-        in_specs=[VMEM, VMEM],
-        out_specs=(VMEM, VMEM),
-        scratch_shapes=[
-            pltpu.VMEM((NX, NZ, rows, cols), f32),
-            pltpu.VMEM((NX, NZ, rows, cols), f32),
-            pltpu.VMEM((NX - 1, NZ, rows, half), f32),
-            pltpu.VMEM((NZ - 1, NX, rows, half), f32),
-            pltpu.VMEM((NZ - 1, rows, half), f32),
-            pltpu.VMEM((NX - 1, rows, half), f32),
-            pltpu.VMEM((NZ, rows, half), f32),
-            pltpu.VMEM((NX, rows, half), f32),
-            pltpu.VMEM((rows, cols), f32),
-            pltpu.VMEM((NY - 1, rows, cols), f32),
-            pltpu.VMEM((PLANE, grows, cols), f32),
-            pltpu.VMEM((grows, cols), f32),
-            pltpu.VMEM((NY - 1, grows, cols), f32),
-            dma((NX,)), dma((NX,)), dma((4, NX - 1)), dma((4, NX - 1)), dma((NY - 1,)), dma((NY - 1,)),
-            dma((PLANE,)), dma((PLANE,)), dma((NY - 1,)), dma((NY - 1,)), dma((PLANE,)), dma((PLANE,)),
-        ],
-        compiler_params=pltpu.CompilerParams(collective_id=number, has_side_effects=True, vmem_limit_bytes=LIMIT),
-        name="reduce_sums",
-    )(part.reshape(NX, NZ, NCORE, rows, cols), gram.reshape(PLANE, grows, cols))
-    return out, summed.reshape(gram.shape)
-
-
 BLOCK = 64
 
 
@@ -406,39 +277,167 @@
     return m * (1.0 / jnp.sqrt(diag))
 
 
-def inverse_factor_kernel(gram_ref, out_ref, work):
-    n = gram_ref.shape[0]
-    work[:, 0:n] = gram_ref[...]
+def factor_start(gram, work):
+    n = gram.shape[0]
+    work[:, 0:n] = gram
     row = lax.broadcasted_iota(jnp.int32, (n, n), 0)
     col = lax.broadcasted_iota(jnp.int32, (n, n), 1)
     work[:, n:] = jnp.where(row == col, 1.0, 0.0)
+
+
+def factor_block(low, work, out_ref):
+    n = out_ref.shape[0]
+    high = low + BLOCK
     brow = lax.broadcasted_iota(jnp.int32, (BLOCK, BLOCK), 0)
     bcol = lax.broadcasted_iota(jnp.int32, (BLOCK, BLOCK), 1)
     unit = jnp.where(brow == bcol, 1.0, 0.0)
-    for low in range(0, n, BLOCK):
-        high = low + BLOCK
-        block = work[low:high, low:high]
-        inv = eliminated(jnp.concatenate([block, unit], axis=1))[:, BLOCK:]
-        scaled = jnp.dot(inv, work[low:high, :], precision=HIGHEST, preferred_element_type=jnp.float32)
-        out_ref[low:high, :] = scaled[:, n:]
-        if high < n:
-            lower = scaled[:, high:n]
-            update = lax.dot_general(
-                lower, scaled, (((0,), (0,)), ((), ())), precision=HIGHEST, preferred_element_type=jnp.float32
-            )
-            work[high:, :] = work[high:, :] - update
-
-
-def inverse_factor(gram):
-    n = gram.shape[0]
+    block = work[low:high, low:high]
+    inv = eliminated(jnp.concatenate([block, unit], axis=1))[:, BLOCK:]
+    scaled = jnp.dot(inv, work[low:high, :], precision=HIGHEST, preferred_element_type=jnp.float32)
+    out_ref[low:high, :] = scaled[:, n:]
+    if high < n:
+        lower = scaled[:, high:n]
+        update = lax.dot_general(
+            lower, scaled, (((0,), (0,)), ((), ())), precision=HIGHEST, preferred_element_type=jnp.float32
+        )
+        work[high:, :] = work[high:, :] - update
+
+
+def reduce_kernel(
+    part_ref, gram_ref, rows_ref, inverse_ref,
+    from_twin, both, over_x, over_z, late_z, late_x, stage0, stage1, plane_sum, from_y,
+    gram_in, gram_rows, gram_y, out_gram_ref, work,
+    twin_send, twin_recv, send, recv, ysend, yrecv, gsend, grecv, gysend, gyrecv, bsend, brecv,
+):
+    me, x, z, c = place()
+    y = lax.axis_index("grid")
+    half = rows_ref.shape[1] // 2
+    left, right = pl.ds(0, half), pl.ds(half, half)
+    xs = [((x + k) % NX) for k in range(1, NX)]
+    zs = [((z + k) % NZ) for k in range(1, NZ)]
+    xpeers = [{"ens": v * NZ * NCORE + z * NCORE + c} for v in xs]
+    zpeers = [{"ens": x * NZ * NCORE + v * NCORE + c} for v in zs]
+    ypeers = [{"grid": (y + k) % NY} for k in range(1, NY)]
+    twin = {"ens": me + 1 - 2 * c}
+    greet_plane(me, ypeers)
+
+    def gram_copy(k):
+        peer = (me + k) % PLANE
+        return remote(gram_ref.at[peer], gram_in.at[me], gsend.at[k], grecv.at[k], {"ens": peer})
+
+    each(1, PLANE, lambda k: gram_copy(k).start())
+    order = xs + [x]
+    halves = [
+        remote(part_ref.at[v, :, 1 - c], from_twin.at[v], twin_send.at[i], twin_recv.at[i], twin)
+        for i, v in enumerate(order)
+    ]
+    for copy in halves:
+        copy.start()
+    gram_in[me] = gram_ref[me]
+    each(1, PLANE, lambda k: gram_copy(k).wait())
+    gram_rows[...] = jnp.sum(gram_in[...], axis=0)
+    gram_over_y = [
+        remote(gram_rows, gram_y.at[y], gysend.at[k], gyrecv.at[k], ypeers[k]) for k in range(NY - 1)
+    ]
+    for copy in gram_over_y:
+        copy.start()
+    for copy in gram_over_y:
+        copy.wait()
+    gram_y[y] = gram_rows[...]
+    out_gram_ref[me] = jnp.sum(gram_y[...], axis=0)
+
+    def gram_back(k):
+        return remote(out_gram_ref.at[me], out_gram_ref.at[me], bsend.at[k], brecv.at[k], {"ens": (me + k) % PLANE})
+
+    each(1, PLANE, lambda k: gram_back(k).start())
+    x_first = []
+    for i, v in enumerate(order):
+        halves[i].wait()
+        both[v] = part_ref[v, :, c] + from_twin[v]
+        if i < NX - 1:
+            copy = remote(both.at[v, :, :, left], over_x.at[i], send.at[0, i], recv.at[0, i], xpeers[i])
+            copy.start()
+            x_first.append(copy)
+    z_first = []
+    for i, v in enumerate(zs):
+        copy = remote(both.at[:, v, :, right], over_z.at[i], send.at[1, i], recv.at[1, i], zpeers[i])
+        copy.start()
+        z_first.append(copy)
+    each(1, PLANE, lambda k: gram_back(k).wait())
+    n = inverse_ref.shape[0]
+    factor_start(out_gram_ref[...].reshape(n, n), work)
+    factor_block(0, work, inverse_ref)
+    factor_block(BLOCK, work, inverse_ref)
+    for copy in x_first:
+        copy.wait()
+    stage0[...] = both[x, :, :, 0:half] + over_x[0] + over_x[1] + over_x[2]
+    second = [
+        remote(stage0.at[v], late_z.at[i], send.at[2, i], recv.at[2, i], zpeers[i]) for i, v in enumerate(zs)
+    ]
+    for copy in second:
+        copy.start()
+    for copy in z_first:
+        copy.wait()
+    stage1[...] = both[:, z, :, half:] + over_z[0] + over_z[1] + over_z[2]
+    third = [
+        remote(stage1.at[v], late_x.at[i], send.at[3, i], recv.at[3, i], xpeers[i]) for i, v in enumerate(xs)
+    ]
+    for copy in third:
+        copy.start()
+    factor_block(2 * BLOCK, work, inverse_ref)
+    for copy in second:
+        copy.wait()
+    plane_sum[:, 0:half] = stage0[z] + late_z[0] + late_z[1] + late_z[2]
+    for copy in third:
+        copy.wait()
+    plane_sum[:, half:] = stage1[x] + late_x[0] + late_x[1] + late_x[2]
+    over_y = [remote(plane_sum, from_y.at[y], ysend.at[k], yrecv.at[k], ypeers[k]) for k in range(NY - 1)]
+    for copy in over_y:
+        copy.start()
+    factor_block(3 * BLOCK, work, inverse_ref)
+    for copy in over_y:
+        copy.wait()
+    from_y[y] = plane_sum[...]
+    rows_ref[...] = jnp.sum(from_y[...], axis=0)
+
+
+def reduce_sums(part, gram, number):
+    total, cols = part.shape
+    rows = total // PLANE
+    half = cols // 2
+    grows = gram.shape[0] // PLANE
+    f32 = jnp.float32
+    dma = pltpu.SemaphoreType.DMA
     return pl.pallas_call(
-        inverse_factor_kernel,
-        out_shape=jax.ShapeDtypeStruct((n, n), jnp.float32),
-        in_specs=[VMEM],
-        out_specs=VMEM,
-        scratch_shapes=[pltpu.VMEM((n, 2 * n), jnp.float32)],
-        name="inverse_factor",
-    )(gram)
+        reduce_kernel,
+        out_shape=(
+            jax.ShapeDtypeStruct((rows, cols), f32),
+            jax.ShapeDtypeStruct(gram.shape, f32),
+        ),
+        in_specs=[VMEM, VMEM],
+        out_specs=(VMEM, VMEM),
+        scratch_shapes=[
+            pltpu.VMEM((NX, NZ, rows, cols), f32),
+            pltpu.VMEM((NX, NZ, rows, cols), f32),
+            pltpu.VMEM((NX - 1, NZ, rows, half), f32),
+            pltpu.VMEM((NZ - 1, NX, rows, half), f32),
+            pltpu.VMEM((NZ - 1, rows, half), f32),
+            pltpu.VMEM((NX - 1, rows, half), f32),
+            pltpu.VMEM((NZ, rows, half), f32),
+            pltpu.VMEM((NX, rows, half), f32),
+            pltpu.VMEM((rows, cols), f32),
+            pltpu.VMEM((NY, rows, cols), f32),
+            pltpu.VMEM((PLANE, grows, cols), f32),
+            pltpu.VMEM((grows, cols), f32),
+            pltpu.VMEM((NY, grows, cols), f32),
+            pltpu.VMEM((PLANE, grows, cols), f32),
+            pltpu.VMEM((gram.shape[0], 2 * gram.shape[0]), f32),
+            dma((NX,)), dma((NX,)), dma((4, NX - 1)), dma((4, NX - 1)), dma((NY - 1,)), dma((NY - 1,)),
+            dma((PLANE,)), dma((PLANE,)), dma((NY - 1,)), dma((NY - 1,)), dma((PLANE,)), dma((PLANE,)),
+        ],
+        compiler_params=pltpu.CompilerParams(collective_id=number, has_side_effects=True, vmem_limit_bytes=LIMIT),
+        name="reduce_sums",
+    )(part.reshape(NX, NZ, NCORE, rows, cols), gram.reshape(PLANE, grows, cols))
 
 
 def product(fields, span):
@@ -472,11 +471,10 @@
     fields = fields.reshape(-1, fields.shape[2])
 
     first_span = span_of(fields, mixing)
-    rows, gram = reduce_sums(product(fields, first_span), gram_of(first_span), 2)
-    weights = times_inverse_transposed(rows, inverse_factor(gram)).astype(jnp.bfloat16)
+    rows, inverse = reduce_sums(product(fields, first_span), gram_of(first_span), 2)
+    weights = times_inverse_transposed(rows, inverse).astype(jnp.bfloat16)
     second_span = span_of(fields, gather(weights, 3))
-    rows, gram = reduce_sums(product(fields, second_span), gram_of(second_span), 4)
-    inverse = inverse_factor(gram)
+    rows, inverse = reduce_sums(product(fields, second_span), gram_of(second_span), 4)
     basis = times_inverse_transposed(second_span, inverse) * math.sqrt(total_cells)
     coefficients = times_inverse_transposed(rows, inverse) * math.sqrt(rank_width / total_cells)
     return (basis, coefficients)

time: 222 us -> 215 us (0.968)
  Pallas kernels: 196 us -> 188 us
    pallas_call x2 -> x0, Pallas kernels: 34.4 us -> none  [inverse_factor(): pl.pallas_call(inverse_factor_kernel, out_shape=jax.ShapeDtypeStruct((n,...]
    pallas_call x2, Pallas kernels: 85.3 us -> 110 us  [reduce_sums(): pl.pallas_call(reduce_kernel, out_shape=(jax.ShapeDtypeStruct((rows, cols...]
where the time goes in v3:
time: 215 us; the launch traced here: 214 us
  Pallas kernels  188 us (87%)
  matrix products  14.6 us (7%)
  other arithmetic  9.21 us (4%)
    pallas_call x2, Pallas kernels, reduce_sums(): pl.pallas_call(reduce_kernel, out_shape=(jax.ShapeDtypeStruct((rows, cols...  110 us
    pallas_call x1, Pallas kernels, spread(): pl.pallas_call(spread_kernel, out_shape=(jax.ShapeDtypeStruct((PLANE, sce...  58 us
    pallas_call x1, Pallas kernels, gather(): pl.pallas_call(gather_kernel, out_shape=jax.ShapeDtypeStruct((NX, NZ, NCO...  20.2 us
    dot_general x3, matrix products, times_inverse_transposed(): lax.dot_general(rows, inverse, (((1,), (1,)), ((), ())), precision=HIGHEST)  6.37 us
    add x2, other arithmetic, product(): return both[:, :cols] + both[:, cols:]  4.96 us

profile of v3, /device:TPU:0, one launch (start us, length us, event | category | flops | bytes accessed | tf_op | source)
XLA Modules:
  0.0 213.9 jit_solution(17499149045161384909)
XLA Ops:
  0.6 1.4 copy.6.mask_ref
  2.0 58.0 %spread.1 = (bf16[32,128,256]{2,1,0:T(8,128)(2,1)}, f32[32,8,256]{2,1,0:T(8,128)}, bf16[4,4,2,128,256]{4,3,2,1,0:T(8,128)(2,1)}) custom-call(bf16[128,8192]{1,0:T(8,128)(2,1)} %snap_ref.1, s32[16,5]{1,0:T(8,128)} %copy.6.mask_ref, bf16[5,512,512]{2,1,0:T(8,128)(2,1)} %kernels_ref.1, bf16[128,256]{1,0:T(8,128)(2,1)} %mix_ref.1), custom_call_target="tpu_custom_call" | custom-call | tf_op jit(solution)/shard_map/spread/pallas_call | solution.py:178
  60.0 1.0 slice_reduce_fusion
  61.0 1.0 slice_subtract_fusion
  62.0 0.0 copy-start
  62.0 2.3 %add_convert_fusion = bf16[32,128,256]{2,1,0:T(8,128)(2,1)S(1)} fusion(bf16[32,128,256]{2,1,0:T(8,128)(2,1)} %get-tuple-element.9, f32[32,256]{1,0:T(8,128)S(1)} %bitcast.35), kind=kLoop, calls=%fused_computation.2 | loop fusion | flops 3145728 | bytes 4227072 | tf_op jit(solution)/shard_map/convert_element_type | solution.py:470
  64.3 0.0 copy-done
  64.3 1.0 subtract_convert_fusion.1
  65.3 1.1 convolution_bitcast_fusion.1.gram_ref
  66.4 1.3 fusion
  67.7 2.5 %slice_add_fusion.1 = f32[4096,256]{1,0:T(8,128)} fusion(f32[4096,512]{1,0:T(8,128)S(1)} %fusion), kind=kLoop, calls=%fused_computation.1 | loop fusion | flops 1048576 | bytes 12582912 | tf_op jit(solution)/shard_map/add | solution.py:448
  70.2 56.9 %reduce_sums.2 = (f32[128,256]{1,0:T(8,128)}, f32[256,256]{1,0:T(8,128)}) custom-call(f32[4,4,2,128,256]{4,3,2,1,0:T(8,128)} %bitcast.32, f32[32,8,256]{2,1,0:T(8,128)} %convolution_bitcast_fusion.1.gram_ref), custom_call_target="tpu_custom_call" | custom-call | tf_op jit(solution)/shard_map/reduce_sums/pallas_call | solution.py:411
  127.1 2.1 convolution_convert_fusion.own_ref
  129.1 20.2 %gather_rows.1 = bf16[4,4,2,128,256]{4,3,2,1,0:T(8,128)(2,1)} custom-call(bf16[128,256]{1,0:T(8,128)(2,1)} %convolution_convert_fusion.own_ref), custom_call_target="tpu_custom_call" | custom-call | tf_op jit(solution)/shard_map/gather_rows/pallas_call | solution.py:236
  149.3 2.5 %subtract_convert_fusion = (bf16[256,256]{0,1:T(8,128)(2,1)S(1)}, bf16[256,256]{0,1:T(8,128)(2,1)S(1)}, f32[256,256]{0,1:T(8,128)S(1)}) fusion(bf16[4096,256]{1,0:T(8,128)(2,1)S(1)} %bitcast.30, bf16[4096,256]{1,0:T(8,128)(2,1)} %bitcast.34), kind=kOutput, calls=%fused_computation.16 | convolution fusion | flops 537133056 | bytes 4718592 | tf_op jit(solution)/shard_map/dot_general | solution.py:452
  151.8 1.1 convolution_bitcast_fusion.gram_ref
  153.0 1.3 fusion.4
  154.2 2.5 %slice_add_fusion = f32[4096,256]{1,0:T(8,128)} fusion(f32[4096,512]{1,0:T(8,128)S(1)} %fusion.4), kind=kLoop, calls=%fused_computation | loop fusion | flops 1048576 | bytes 12582912 | tf_op jit(solution)/shard_map/add | solution.py:448
  156.7 52.9 %reduce_sums.3 = (f32[128,256]{1,0:T(8,128)}, f32[256,256]{1,0:T(8,128)}) custom-call(f32[4,4,2,128,256]{4,3,2,1,0:T(8,128)} %bitcast.33, f32[32,8,256]{2,1,0:T(8,128)} %convolution_bitcast_fusion.gram_ref), custom_call_target="tpu_custom_call" | custom-call | tf_op jit(solution)/shard_map/reduce_sums/pallas_call | solution.py:411
  209.6 2.1 convolution_multiply_fusion.1
  211.7 2.2 %convolution_multiply_fusion = f32[256,256]{1,0:T(8,128)} fusion(f32[256,256]{0,1:T(8,128)S(1)} %get-tuple-element.21, f32[256,256]{1,0:T(8,128)} %get-tuple-element.14), kind=kOutput, calls=%fused_computation.3 | convolution fusion | flops 201392128 | bytes 786432 | tf_op jit(solution)/shard_map/dot_general | solution.py:460
  (2 shorter events, 0.0 us)
Async XLA Ops:
  62.0 2.3 %copy-start = (bf16[4,4,2,128,256]{4,3,2,1,0:T(8,128)(2,1)S(1)}, bf16[4,4,2,128,256]{4,3,2,1,0:T(8,128)(2,1)}, u32[]{:S(2)}) copy-start(bf16[4,4,2,128,256]{4,3,2,1,0:T(8,128)(2,1)} %get-tuple-element.11) | copy-start | bytes 6291460
